TPU v7x, 32 devices: a whole 2x2x4 slice. The times are simulated.
32 devices in a mesh: cam: 2 (over core), tile: 16 (over z, y, x).
Axes of the slice: x: 2, y: 2, z: 4, core: 2. Of those that a mesh axis runs over, the one named last changes fastest.
Arguments:
- queries: bfloat16 [4096, 256], P('tile'), as said below
- keys: bfloat16 [2048, 256], P(('cam', 'tile')), as said below
- values: bfloat16 [2048, 256], P(('cam', 'tile')), may hold values from -6 to 6
- grad_out: bfloat16 [4096, 256], P('tile'), may hold values from -6 to 6
- visible: int32 [32, 64], P('tile', 'cam'), may hold values from 0 to 1, as said below
- counts: int32 [64], P('cam'), may hold values from 2 to 32
Outputs:
- grad_queries: bfloat16 [4096, 256], P('tile')
- grad_keys: bfloat16 [2048, 256], P(('cam', 'tile'))
- grad_values: bfloat16 [2048, 256], P(('cam', 'tile'))
Inputs may be any that keep to these rules, and one draw needn't show every extreme that they name: Every tile has at least one visible block. `queries`: projected query features. `keys`: projected key features.
All inputs are finite; a program needn't handle non-finite values.
Results may differ from a plain program's by a relative error of at most 0.0052.
Values may be sent and summed in bfloat16 or wider, within the bound.
No kernel may reach another device: no remote copies, remote signals or barrier semaphores. Data moves between devices by JAX's collectives and lax.ppermute only.
A program may use at most 128 MiB of HBM per device.

v0:
```python
import math
import jax
import jax.numpy as jnp
from jax import lax
from jax.sharding import PartitionSpec as P

H = 8


def merged(array, axis, combine):
    everything = jax.tree.map(lambda part: lax.all_gather(part, axis), array)
    initial = jax.tree.map(lambda part: part[0], everything)

    def step(k, so_far):
        return combine(so_far, jax.tree.map(lambda part: part[k], everything))

    return lax.fori_loop(1, lax.axis_size(axis), step, initial)


def combine_stats(first, second):
    top = jnp.maximum(first[0], second[0])
    total = first[1] * jnp.exp(first[0] - top) + second[1] * jnp.exp(second[0] - top)
    return (top, total)


def shards(queries, keys, values, grad_out, visible, counts):
    row_count, width = queries.shape
    head_dim = width // H
    scale = 1.0 / math.sqrt(head_dim)
    key_all, value_all = (
        lax.all_gather(keys, "tile", axis=0, tiled=True),
        lax.all_gather(values, "tile", axis=0, tiled=True),
    )
    group = key_all.shape[0]
    block_count = counts.shape[0]
    block_keys = group // block_count
    slot_index = jnp.arange(group, dtype=jnp.int32) % block_keys
    key_valid = slot_index < jnp.repeat(counts, block_keys)
    tile_count = visible.shape[0]
    tile_rows = row_count // tile_count
    mask_tiles = (jnp.repeat(visible, block_keys, axis=1) == 1) & key_valid[None, :]
    per_step = 2
    step_count = tile_count // per_step
    step_rows = per_step * tile_rows
    query_blocks = queries.reshape(step_count, step_rows, H, head_dim)
    grad_blocks = grad_out.reshape(step_count, step_rows, H, head_dim)
    mask_blocks = mask_tiles.reshape(step_count, per_step, group)
    key_heads = key_all.reshape(group, H, head_dim)
    value_heads = value_all.reshape(group, H, head_dim)

    def scores_of(query_blk, key_mat):
        return (
            jnp.einsum("qhd,khd->hqk", query_blk, key_mat, preferred_element_type=jnp.float32)
            * scale
        )

    def row_mask(mask_blk):
        return jnp.repeat(mask_blk, tile_rows, axis=0)[None, :, :]

    def local_stats(inputs):
        query_blk, mask_blk = inputs
        scores = scores_of(query_blk, key_heads)
        allowed = row_mask(mask_blk)
        top = jnp.max(jnp.where(allowed, scores, -1e30), axis=-1)
        total = jnp.sum(jnp.where(allowed, jnp.exp(scores - top[..., None]), 0.0), axis=-1)
        return (top, total)

    local_top, local_total = lax.map(local_stats, (query_blocks, mask_blocks))
    global_top, global_total = merged((local_top, local_total), "cam", combine_stats)
    lse_all = global_top + jnp.log(global_total)

    def probs_terms(query_blk, grad_blk, mask_blk, lse_blk, key_mat, value_mat):
        scores = scores_of(query_blk, key_mat)
        allowed = row_mask(mask_blk)
        probs = jnp.where(allowed, jnp.exp(scores - lse_blk[..., None]), 0.0)
        dprobs = jnp.einsum("qhd,khd->hqk", grad_blk, value_mat, preferred_element_type=jnp.float32)
        return (probs, dprobs)

    def local_delta(inputs):
        query_blk, grad_blk, mask_blk, lse_blk = inputs
        probs, dprobs = probs_terms(query_blk, grad_blk, mask_blk, lse_blk, key_heads, value_heads)
        return jnp.sum(probs * dprobs, axis=-1)

    delta_part = lax.map(local_delta, (query_blocks, grad_blocks, mask_blocks, lse_all))
    delta_all = lax.psum(delta_part, "cam")

    def rounded_terms(query_blk, grad_blk, mask_blk, lse_blk, delta_blk, key_mat, value_mat):
        probs, dprobs = probs_terms(query_blk, grad_blk, mask_blk, lse_blk, key_mat, value_mat)
        dscores = probs * (dprobs - delta_blk[..., None])
        return (probs.astype(jnp.bfloat16), dscores.astype(jnp.bfloat16))

    def query_grad_of(dscores_b):
        grad_q = (
            jnp.einsum("hqk,khd->qhd", dscores_b, key_heads, preferred_element_type=jnp.float32)
            * scale
        )
        return grad_q.reshape(step_rows, width)

    def grad_step(carry, inputs):
        query_blk, grad_blk, mask_blk, lse_blk, delta_blk = inputs
        probs_b, dscores_b = rounded_terms(
            query_blk, grad_blk, mask_blk, lse_blk, delta_blk, key_heads, value_heads
        )
        grad_k = (
            carry[0]
            + jnp.einsum("hqk,qhd->khd", dscores_b, query_blk, preferred_element_type=jnp.float32)
            * scale
        )
        grad_v = carry[1] + jnp.einsum(
            "hqk,qhd->khd", probs_b, grad_blk, preferred_element_type=jnp.float32
        )
        return ((grad_k, grad_v), query_grad_of(dscores_b))

    zero_kv = jnp.zeros((group, H, head_dim), jnp.float32)
    (grad_k, grad_v), query_parts = lax.scan(
        grad_step, (zero_kv, zero_kv), (query_blocks, grad_blocks, mask_blocks, lse_all, delta_all)
    )
    joined = jnp.concatenate((grad_k.reshape(group, width), grad_v.reshape(group, width)), axis=1)
    owned = lax.psum_scatter(joined, "tile", scatter_dimension=0, tiled=True)
    grad_queries = lax.psum(query_parts.reshape(row_count, width), "cam").astype(jnp.bfloat16)
    grad_keys = owned[:, :width].astype(jnp.bfloat16)
    grad_values = owned[:, width:].astype(jnp.bfloat16)
    return (grad_queries, grad_keys, grad_values)


def solution(mesh):
    in_specs = (
        P("tile", None),
        P(("cam", "tile"), None),
        P(("cam", "tile"), None),
        P("tile", None),
        P("tile", "cam"),
        P("cam"),
    )
    out_specs = (P("tile", None), P(("cam", "tile"), None), P(("cam", "tile"), None))
    return jax.shard_map(shards, mesh=mesh, in_specs=in_specs, out_specs=out_specs, check_vma=False)
```

profile of v0, /device:TPU:0, one launch (start us, length us, event | category | flops | bytes accessed | tf_op | source)
XLA Modules:
  0.0 218.7 jit_solution(8810301855245995741)
XLA Ops:
  7.2 0.7 broadcast_in_dim.79
  7.9 0.1 reshape.121
  8.0 0.7 broadcast_compare_fusion
  8.7 0.1 broadcast_in_dim.78
  8.8 0.1 eq.14
  8.9 45.6 %all_gather.18 = bf16[1024,256]{1,0:T(8,128)(2,1)S(1)} all-gather(bf16[64,256]{1,0:T(8,128)(2,1)} %param.7), channel_id=1, replica_groups=mesh['cam'=2,'tile'=16] {'tile'}, dimensions={0}, use_global_device_ids=true | all-gather | bytes 557056 | tf_op jit(solution)/shard_map/all_gather | solution.py:31
  54.4 0.2 copy.19
  54.7 1.0 copy.18
  55.8 1.7 select_reduce_fusion.1
  57.5 1.8 all-gather
  59.3 1.4 copy-done
  60.7 2.4 %select_reduce_fusion = f32[8,256]{1,0:T(8,128)S(1)} fusion(f32[8,256,1024]{2,1,0:T(8,128)S(1)} %get-tuple-element.69, f32[8,256]{1,0:T(8,128)S(1)} %get-tuple-element.68, pred[256,1024]{1,0:T(8,128)(4,1)S(1)} %bitcast.24), kind=kLoop, calls=%fused_computation.3 | loop fusion | flops 8386560 | bytes 8667136 | tf_op jit(solution)/shard_map/while/body/eval_jaxpr/reduce_sum | solution.py:65
  63.1 1.8 all-gather.1
  64.9 0.1 copy.20
  65.1 38.3 %all_gather.23 = bf16[1024,256]{1,0:T(8,128)(2,1)S(1)} all-gather(bf16[64,256]{1,0:T(8,128)(2,1)S(1)} %copy-done.4), channel_id=1, replica_groups=mesh['cam'=2,'tile'=16] {'tile'}, dimensions={0}, use_global_device_ids=true | all-gather | bytes 557056 | tf_op jit(solution)/shard_map/all_gather | solution.py:32
  103.3 0.2 copy.21
  103.6 5.7 %fusion.1 = f32[8,1024,32]{1,2,0:T(8,128)} fusion(bf16[256,8,32]{0,2,1:T(8,128)(2,1)S(1)} %bitcast.36, f32[8,256,1024]{2,1,0:T(8,128)} %copy-done, f32[8,256]{1,0:T(8,128)S(1)} %fusion.6, pred[256,1024]{1,0:T(8,128)(4,1)S(1)} %bitcast.25), kind=kOutput, calls=%fused_computation.6 | convolution fusion | flops 142606336 | bytes 9838592 | tf_op jit(solution)/shard_map/while/body/eval_jaxpr/hqk,qhd->khd/dot_general | solution.py:109
  109.3 0.3 copy-done.1
  109.6 5.4 %multiply_reduce_fusion = (f32[8,256]{1,0:T(8,128)S(1)}, f32[8,256,1024]{2,1,0:T(8,128)}) fusion(f32[8,256,1024]{2,1,0:T(8,128)S(1)} %copy-done.1, f32[8,256]{1,0:T(8,128)S(1)} %fusion.6, pred[256,1024]{1,0:T(8,128)(4,1)S(1)} %bitcast.26, bf16[256,8,32]{0,2,1:T(8,128)(2,1)S(1)} %bitcast.37, bf16[1024,8,32]{0,2,1:T(8,128)(2,1)S(1)} %bitcast.31), kind=kOutput, calls=%fused_computation.1 | convolution fusion | flops 144701440 | bytes 17711104 | tf_op jit(solution)/shard_map/while/body/eval_jaxpr/qhd,khd->hqk/dot_general | solution.py:76
  114.9 2.5 %psum.14 = f32[8,256]{1,0:T(8,128)S(1)} all-reduce(f32[8,256]{1,0:T(8,128)S(1)} %get-tuple-element.70), channel_id=1, replica_groups=mesh['cam'=2,'tile'=16] {'cam'}, use_global_device_ids=true, to_apply=%region_3.4 | all-reduce | flops 2048 | bytes 16384 | tf_op jit(solution)/shard_map/psum | solution.py:85
  117.4 7.1 %multiply_convert_fusion = bf16[8,256,1024]{2,1,0:T(8,128)(2,1)S(1)} fusion(f32[8,256,1024]{2,1,0:T(8,128)} %get-tuple-element.71, f32[8,256,1024]{2,1,0:T(8,128)} %copy-done, f32[8,256]{1,0:T(8,128)S(1)} %psum.14, f32[8,256]{1,0:T(8,128)S(1)} %fusion.6, pred[256,1024]{1,0:T(8,128)(4,1)S(1)} %bitcast.27), kind=kLoop, calls=%fused_computation | loop fusion | flops 12582912 | bytes 21250048 | tf_op jit(solution)/shard_map/while/body/eval_jaxpr/convert_element_type | solution.py:90
  124.5 1.9 copy-done.2
  126.4 0.8 convolution_multiply_fusion
  127.2 0.3 copy.23
  127.6 1.6 copy.24
  129.1 1.7 pad_maximum_fusion
  130.8 3.5 %convolution_multiply_fusion.1 = f32[8,256,32]{1,2,0:T(8,128)S(1)} fusion(bf16[8,256,1024]{2,1,0:T(8,128)(2,1)} %copy-done.2, bf16[1024,8,32]{0,2,1:T(8,128)(2,1)S(1)} %bitcast.29), kind=kOutput, calls=%fused_computation.10 | convolution fusion | flops 134283264 | bytes 4980736 | tf_op jit(solution)/shard_map/while/body/eval_jaxpr/hqk,khd->qhd/dot_general | solution.py:94
  134.3 0.1 copy.22
  134.5 4.7 %all-reduce.1 = bf16[256,256]{1,0:T(8,128)(2,1)} all-reduce(f32[256,256]{1,0:T(8,128)S(1)} %copy.22), channel_id=1, replica_groups=mesh['cam'=2,'tile'=16] {'cam'}, use_global_device_ids=true, to_apply=%region_4.5 | all-reduce | flops 65536 | bytes 393216 | tf_op jit(solution)/shard_map/psum | solution.py:120
  139.2 71.1 %reduce-scatter.2.cloned.1.call-done = f32[64,512]{1,0:T(8,128)} async-done(((f32[1024,512]{1,0:T(8,128)}), f32[64,512]{1,0:T(8,128)}) %reduce-scatter.2.cloned.1.call-update) | async-done | bytes 131088 | tf_op jit(solution)/shard_map/reduce_scatter | solution.py:119
  210.3 0.9 convert.4
  211.2 0.6 fusion.14
  (13 shorter events, 0.2 us)
Async XLA Ops:
  7.2 203.2 %reduce-scatter.2.cloned.1.call-start = ((), (), s32[]{:S(2)}) async-start(), calls=%async_computation.1 | async-start | bytes 2228224 | tf_op jit(solution)/shard_map/reduce_scatter | solution.py:119
  55.8 9.2 %copy-start.3 = (bf16[256,256]{1,0:T(8,128)(2,1)S(1)}, bf16[256,256]{1,0:T(8,128)(2,1)}, u32[]{:S(2)}) copy-start(bf16[256,256]{1,0:T(8,128)(2,1)} %param.9) | copy-start | bytes 393220
  55.8 9.3 %copy-start.4 = (bf16[64,256]{1,0:T(8,128)(2,1)S(1)}, bf16[64,256]{1,0:T(8,128)(2,1)}, u32[]{:S(2)}) copy-start(bf16[64,256]{1,0:T(8,128)(2,1)} %param.8) | copy-start | bytes 98308
  57.5 3.2 %copy-start = (f32[8,256,1024]{2,1,0:T(8,128)}, f32[8,256,1024]{2,1,0:T(8,128)S(1)}, u32[]{:S(2)}) copy-start(f32[8,256,1024]{2,1,0:T(8,128)S(1)} %get-tuple-element.69) | copy-start | bytes 25165828
  103.5 6.0 %copy-start.1 = (f32[8,256,1024]{2,1,0:T(8,128)S(1)}, f32[8,256,1024]{2,1,0:T(8,128)}, u32[]{:S(2)}) copy-start(f32[8,256,1024]{2,1,0:T(8,128)} %copy-done) | copy-start | bytes 25165828
  124.5 1.9 copy-start.2
Sparse Core Ops, SparseCore 0:
  130.9 79.3 reduce-scatter.1
where the time goes:
time: 219 us
  blocking collectives  94.6 us (43%)
  waiting for transfers between devices  71.2 us (33%)
  matrix products  17.1 us (8%)
  between operations  14.2 us (6%)
  other arithmetic  12.8 us (6%)
  local copies, waits for them, and re-layouts  8.84 us (4%)
    reduce_scatter x1, waiting for transfers between devices, shards(): owned = lax.psum_scatter(joined, 'tile', scatter_dimension=0, tiled=True)  71.1 us
    all_gather x1, blocking collectives, shards(): lax.all_gather(keys, 'tile', axis=0, tiled=True)  45.6 us
    all_gather x1, blocking collectives, shards(): lax.all_gather(values, 'tile', axis=0, tiled=True)  38.3 us
    convert_element_type x1, other arithmetic, rounded_terms(): return (probs.astype(jnp.bfloat16), dscores.astype(jnp.bfloat16))  7.09 us
    dot_general x1, matrix products, grad_step(): jnp.einsum('hqk,qhd->khd', probs_b, grad_blk, preferred_element_type=jnp....  5.71 us
    dot_general x1, matrix products, probs_terms(): jnp.einsum('qhd,khd->hqk', grad_blk, value_mat, preferred_element_type=jn...  5.35 us
    unnamed x12, local copies, waits for them, and re-layouts  4.72 us
    psum x1, blocking collectives, shards(): lax.psum(query_parts.reshape(row_count, width), 'cam').astype(jnp.bfloat16)  4.69 us
  transfers between devices with their start and end apart: 1, of which 1 were waited for; matrix products, arithmetic and copies ran while one was open for 2% of the time, Pallas kernels for 0%

commit v1 on v0

--- a/solution.py
+++ b/solution.py
@@ -1,10 +1,29 @@
+import functools
 import math
 import jax
 import jax.numpy as jnp
 from jax import lax
 from jax.sharding import PartitionSpec as P
+from jax.lax import axis_index, axis_size, ppermute
 
 H = 8
+
+
+def take_the_halves(own_rows, axis_tag):
+    lower, opened = (axis_size(axis_tag), axis_index(axis_tag))
+    f_now, built = (own_rows, 1)
+    while built < lower:
+        mat_out = ppermute(
+            f_now, axis_name=axis_tag, perm=[(tick, tick ^ built) for tick in range(lower)]
+        )
+        y1 = jnp.concatenate([f_now, mat_out], 0)
+        answer = jnp.concatenate([mat_out, f_now], axis=0)
+        f_now = jnp.where(opened & built == 0, y1, answer)
+        built = 2 * built
+    return f_now
+
+
+view_derive = functools.partial(take_the_halves, axis_tag="tile")
 
 
 def merged(array, axis, combine):
@@ -27,10 +46,7 @@
     row_count, width = queries.shape
     head_dim = width // H
     scale = 1.0 / math.sqrt(head_dim)
-    key_all, value_all = (
-        lax.all_gather(keys, "tile", axis=0, tiled=True),
-        lax.all_gather(values, "tile", axis=0, tiled=True),
-    )
+    key_all, value_all = (view_derive(keys), lax.all_gather(values, "tile", axis=0, tiled=True))
     group = key_all.shape[0]
     block_count = counts.shape[0]
     block_keys = group // block_count

time: 219 us -> 186 us (0.85)
  blocking collectives: 94.6 us -> 54.5 us
  starting transfers between devices: 0.04 us -> 7.04 us
  waiting for transfers between devices: 71.2 us -> 77.3 us
  matrix products: 17.1 us -> 12.5 us
    all_gather x1 -> x0, blocking collectives: 45.6 us -> none  [shards(): lax.all_gather(keys, 'tile', axis=0, tiled=True)]
    ppermute x0 -> x4, waiting for transfers between devices: none -> 7.54 us  [take_the_halves(): ppermute(f_now, axis_name=axis_tag, perm=[(tick, tick ^ built) for tick i...]
    ppermute x0 -> x4, starting transfers between devices: none -> 7.01 us  [take_the_halves(): ppermute(f_now, axis_name=axis_tag, perm=[(tick, tick ^ built) for tick i...]
    all_gather x1, blocking collectives: 38.3 us -> 43.7 us  [shards(): lax.all_gather(values, 'tile', axis=0, tiled=True)]
    dot_general x1, matrix products: 5.71 us -> 1.78 us  [grad_step(): jnp.einsum('hqk,qhd->khd', probs_b, grad_blk, preferred_element_type=jnp....]
    unnamed x12 -> x9, local copies, waits for them, and re-layouts: 4.72 us -> 4.81 us
  transfers between devices with their start and end apart: 1 -> 5, of which waited for: 1 -> 3; matrix products, arithmetic and copies ran while one was open for 2% -> 4% of each run, Pallas kernels for 0% -> 0%
where the time goes in v1:
time: 186 us
  waiting for transfers between devices  77.3 us (42%)
  blocking collectives  54.5 us (29%)
  between operations  14.2 us (8%)
  other arithmetic  12.6 us (7%)
  matrix products  12.5 us (7%)
  local copies, waits for them, and re-layouts  7.93 us (4%)
  starting transfers between devices  7.04 us (4%)
    reduce_scatter x1, waiting for transfers between devices, shards(): owned = lax.psum_scatter(joined, 'tile', scatter_dimension=0, tiled=True)  69.7 us
    all_gather x1, blocking collectives, shards(): lax.all_gather(values, 'tile', axis=0, tiled=True)  43.7 us
    ppermute x4, waiting for transfers between devices, take_the_halves(): ppermute(f_now, axis_name=axis_tag, perm=[(tick, tick ^ built) for tick i...  7.54 us
    convert_element_type x1, other arithmetic, rounded_terms(): return (probs.astype(jnp.bfloat16), dscores.astype(jnp.bfloat16))  7.04 us
    ppermute x4, starting transfers between devices, take_the_halves(): ppermute(f_now, axis_name=axis_tag, perm=[(tick, tick ^ built) for tick i...  7.01 us
    unnamed x9, local copies, waits for them, and re-layouts  4.81 us
    dot_general x1, matrix products, probs_terms(): jnp.einsum('qhd,khd->hqk', grad_blk, value_mat, preferred_element_type=jn...  4.76 us
    psum x1, blocking collectives, shards(): lax.psum(query_parts.reshape(row_count, width), 'cam').astype(jnp.bfloat16)  4.68 us
  transfers between devices with their start and end apart: 5, of which 3 were waited for; matrix products, arithmetic and copies ran while one was open for 4% of the time, Pallas kernels for 0%

profile of v1, /device:TPU:0, one launch (start us, length us, event | category | flops | bytes accessed | tf_op | source)
XLA Modules:
  0.0 186.1 jit_solution(17042301557115963959)
XLA Ops:
  7.2 0.9 copy.33
  8.1 3.0 %collective-permute-start = (bf16[64,256]{0,1:T(8,128)(2,1)S(1)}, bf16[64,256]{0,1:T(8,128)(2,1)S(1)}, u32[]{:S(2)}, u32[]{:S(2)}) collective-permute-start(bf16[64,256]{0,1:T(8,128)(2,1)S(1)} %copy.33), channel_id=1, source_target_pairs={{0,1},{1,0},{2,3},{3,2},{4,5},{5,4},{6,7},{7,6},{8,9},{9,8},{10,11... | collective-permute-start | bytes 98312 | tf_op jit(solution)/shard_map/ppermute | solution.py:16
  11.1 0.7 broadcast_in_dim.79
  11.9 0.7 broadcast_compare_fusion
  12.8 0.6 collective-permute-done
  13.5 2.1 %collective-permute-start.1 = (bf16[128,256]{0,1:T(8,128)(2,1)S(1)}, bf16[128,256]{0,1:T(8,128)(2,1)S(1)}, u32[]{:S(2)}, u32[]{:S(2)}) collective-permute-start(bf16[128,256]{0,1:T(8,128)(2,1)S(1)} %maximum_select_fusion.8), channel_id=1, source_target_pairs={{0,2},{1,3},{2,0},{3,1},{4,6},{5,7},{6,4},{7,5},{8,10},{9,11},{10,... | collective-permute-start | bytes 196616 | tf_op jit(solution)/shard_map/ppermute | solution.py:16
  15.7 0.4 copy.37
  16.2 1.0 copy.38
  17.2 1.0 copy.39
  18.2 1.8 collective-permute-start.2
  20.0 43.7 %all_gather.19 = bf16[1024,256]{1,0:T(8,128)(2,1)S(1)} all-gather(bf16[64,256]{1,0:T(8,128)(2,1)} %param.8), channel_id=1, replica_groups=mesh['cam'=2,'tile'=16] {'tile'}, dimensions={0}, use_global_device_ids=true | all-gather | bytes 557056 | tf_op jit(solution)/shard_map/all_gather | solution.py:49
  63.7 0.2 copy.40
  64.4 7.0 %collective-permute-done.3 = bf16[512,256]{0,1:T(8,128)(2,1)S(1)} collective-permute-done((bf16[512,256]{0,1:T(8,128)(2,1)S(1)}, bf16[512,256]{0,1:T(8,128)(2,1)S(1)}, u32[]{:S(2)}, u32[]{:S(2)}) %collective-permute-start.3) | collective-permute-done | bytes 262176 | tf_op jit(solution)/shard_map/ppermute | solution.py:16
  71.4 1.6 fusion
  73.0 1.8 all-gather
  74.8 1.7 fusion.3
  76.5 1.8 all-gather.1
  78.4 1.8 fusion.7
  80.2 4.8 %multiply_reduce_fusion = (f32[8,256]{1,0:T(8,128)S(1)}, f32[8,256,1024]{1,2,0:T(8,128)}) fusion(f32[8,1024,256]{2,1,0:T(8,128)S(1)} %get-tuple-element.69, f32[8,256]{1,0:T(8,128)S(1)} %fusion.13, pred[256,1024]{0,1:T(8,128)(4,1)S(1)} %copy.37, bf16[256,8,32]{0,2,1:T(8,128)(2,1)S(1)} %bitcast.55, bf16[1024,8,32]{0,2,1:T(8,128)(2,1)S(1)} %bitcast.49), kind=kOutput, calls=%fused_computation.10 | convolution fusion | flops 144701440 | bytes 17711104 | tf_op jit(solution)/shard_map/while/body/eval_jaxpr/qhd,khd->hqk/dot_general | solution.py:92
  84.9 2.5 %psum.14 = f32[8,256]{1,0:T(8,128)S(1)} all-reduce(f32[8,256]{1,0:T(8,128)S(1)} %get-tuple-element.70), channel_id=1, replica_groups=mesh['cam'=2,'tile'=16] {'cam'}, use_global_device_ids=true, to_apply=%region_3.4 | all-reduce | flops 2048 | bytes 16384 | tf_op jit(solution)/shard_map/psum | solution.py:101
  87.4 7.0 %multiply_convert_fusion = bf16[8,256,1024]{1,2,0:T(8,128)(2,1)S(1)} fusion(f32[8,256,1024]{1,2,0:T(8,128)} %get-tuple-element.71, f32[8,1024,256]{2,1,0:T(8,128)} %copy-done, f32[8,256]{1,0:T(8,128)S(1)} %psum.14, f32[8,256]{1,0:T(8,128)S(1)} %fusion.13, pred[256,1024]{0,1:T(8,128)(4,1)S(1)} %copy.37), kind=kLoop, calls=%fused_computation.9 | loop fusion | flops 12582912 | bytes 21250048 | tf_op jit(solution)/shard_map/while/body/eval_jaxpr/convert_element_type | solution.py:106
  94.4 1.9 %copy-done.1 = bf16[8,256,1024]{1,2,0:T(8,128)(2,1)} copy-done((bf16[8,256,1024]{1,2,0:T(8,128)(2,1)}, bf16[8,256,1024]{1,2,0:T(8,128)(2,1)S(1)}, u32[]{:S(2)}) %copy-start.1) | copy-done | bytes 4194328
  96.4 1.3 convolution_multiply_fusion
  97.7 0.3 copy.47
  98.0 0.3 copy.48
  98.4 1.7 pad_maximum_fusion
  100.0 3.1 %convolution_multiply_fusion.1 = f32[8,32,256]{2,1,0:T(8,128)S(1)} fusion(bf16[8,256,1024]{1,2,0:T(8,128)(2,1)} %copy-done.1, bf16[512,8,32]{0,2,1:T(8,128)(2,1)} %bitcast.60, bf16[512,8,32]{0,2,1:T(8,128)(2,1)S(1)} %maximum_select_fusion.1, pred[]{:T(512)S(6)} %eq.24), kind=kOutput, calls=%fused_computation.16 | convolution fusion | flops 136642560 | bytes 4980737 | tf_op jit(solution)/shard_map/while/body/eval_jaxpr/hqk,khd->qhd/dot_general | solution.py:110
  103.2 0.1 copy.44
  103.3 4.7 %all-reduce.1 = bf16[256,256]{1,0:T(8,128)(2,1)} all-reduce(f32[256,256]{1,0:T(8,128)S(1)} %copy.44), channel_id=1, replica_groups=mesh['cam'=2,'tile'=16] {'cam'}, use_global_device_ids=true, to_apply=%region_4.5 | all-reduce | flops 65536 | bytes 393216 | tf_op jit(solution)/shard_map/psum | solution.py:136
  108.0 69.7 %reduce-scatter.2.cloned.1.call-done = f32[64,512]{1,0:T(8,128)} async-done(((f32[1024,512]{1,0:T(8,128)}), f32[64,512]{1,0:T(8,128)}) %reduce-scatter.2.cloned.1.call-update) | async-done | bytes 131088 | tf_op jit(solution)/shard_map/reduce_scatter | solution.py:135
  177.7 0.9 convert.4
  178.6 0.6 fusion.23
  (23 shorter events, 1.0 us)
Async XLA Ops:
  7.2 170.5 %reduce-scatter.2.cloned.1.call-start = ((), (), s32[]{:S(2)}) async-start(), calls=%async_computation.1 | async-start | bytes 2228224 | tf_op jit(solution)/shard_map/reduce_scatter | solution.py:135
  8.1 5.3 %collective-permute-start = (bf16[64,256]{0,1:T(8,128)(2,1)S(1)}, bf16[64,256]{0,1:T(8,128)(2,1)S(1)}, u32[]{:S(2)}, u32[]{:S(2)}) collective-permute-start(bf16[64,256]{0,1:T(8,128)(2,1)S(1)} %copy.33), channel_id=1, source_target_pairs={{0,1},{1,0},{2,3},{3,2},{4,5},{5,4},{6,7},{7,6},{8,9},{9,8},{10,11... | collective-permute-start | bytes 98312 | tf_op jit(solution)/shard_map/ppermute | solution.py:16
  13.5 4.7 %collective-permute-start.1 = (bf16[128,256]{0,1:T(8,128)(2,1)S(1)}, bf16[128,256]{0,1:T(8,128)(2,1)S(1)}, u32[]{:S(2)}, u32[]{:S(2)}) collective-permute-start(bf16[128,256]{0,1:T(8,128)(2,1)S(1)} %maximum_select_fusion.8), channel_id=1, source_target_pairs={{0,2},{1,3},{2,0},{3,1},{4,6},{5,7},{6,4},{7,5},{8,10},{9,11},{10,... | collective-permute-start | bytes 196616 | tf_op jit(solution)/shard_map/ppermute | solution.py:16
  18.2 45.7 %collective-permute-start.2 = (bf16[256,256]{0,1:T(8,128)(2,1)S(1)}, bf16[256,256]{0,1:T(8,128)(2,1)S(1)}, u32[]{:S(2)}, u32[]{:S(2)}) collective-permute-start(bf16[256,256]{0,1:T(8,128)(2,1)S(1)} %maximum_select_fusion.4), channel_id=1, source_target_pairs={{0,4},{1,5},{2,6},{3,7},{4,0},{5,1},{6,2},{7,3},{8,12},{9,13},{10,... | collective-permute-start | bytes 393224 | tf_op jit(solution)/shard_map/ppermute | solution.py:16
  64.1 7.3 %collective-permute-start.3 = (bf16[512,256]{0,1:T(8,128)(2,1)S(1)}, bf16[512,256]{0,1:T(8,128)(2,1)S(1)}, u32[]{:S(2)}, u32[]{:S(2)}) collective-permute-start(bf16[512,256]{0,1:T(8,128)(2,1)S(1)} %maximum_select_fusion.2), channel_id=1, source_target_pairs={{0,8},{1,9},{2,10},{3,11},{4,12},{5,13},{6,14},{7,15},{8,0},{9,1},... | collective-permute-start | bytes 786440 | tf_op jit(solution)/shard_map/ppermute | solution.py:16
  71.4 16.0 %copy-start.2 = (bf16[512,256]{0,1:T(8,128)(2,1)}, bf16[512,256]{0,1:T(8,128)(2,1)S(1)}, u32[]{:S(2)}) copy-start(bf16[512,256]{0,1:T(8,128)(2,1)S(1)} %collective-permute-done.3) | copy-start | bytes 786436
  73.0 7.2 %copy-start = (f32[8,1024,256]{2,1,0:T(8,128)}, f32[8,1024,256]{2,1,0:T(8,128)S(1)}, u32[]{:S(2)}) copy-start(f32[8,1024,256]{2,1,0:T(8,128)S(1)} %get-tuple-element.69) | copy-start | bytes 25165828
  94.4 1.9 %copy-start.1 = (bf16[8,256,1024]{1,2,0:T(8,128)(2,1)}, bf16[8,256,1024]{1,2,0:T(8,128)(2,1)S(1)}, u32[]{:S(2)}) copy-start(bf16[8,256,1024]{1,2,0:T(8,128)(2,1)S(1)} %multiply_convert_fusion) | copy-start | bytes 12582916
Sparse Core Ops, SparseCore 0:
  100.2 77.4 reduce-scatter.1
